TPU v7x, 32 devices: a whole 2x2x4 slice. The times are simulated.
32 devices in a mesh: req: 8 (over z, y), kv: 4 (over x, core).
Axes of the slice: x: 2, y: 2, z: 4, core: 2. Of those that a mesh axis runs over, the one named last changes fastest.
Arguments:
- tokens: bfloat16 [8, 128, 2880], P('req'), may hold values from -6 to 6
- attn_gain: float32 [2880], replicated, may hold values from 0.1 to 1.9
- w_qkv: bfloat16 [2880, 5120], P(None, 'kv'), may hold values from -0.109375 to 0.109375
- sink_logits: float32 [64], P('kv'), may hold values from 0 to 10
- w_out: bfloat16 [4096, 2880], P('kv'), may hold values from -0.09375 to 0.09375
- kv_cache: bfloat16 [1024, 128, 1024], P('req', None, 'kv'), may hold values from -102 to 102
- page_table: int32 [8, 128], P('req'), may hold values from 0 to 127, each once within a row
- cache_lengths: int32 [8], P('req'), may hold values from 0 to 16384, as said below
- moe_gain: float32 [2880], replicated, may hold values from 0.1 to 1.9
- routes: int32 [8, 128, 4], P('req'), may hold values from 0 to 15, all different within a row; in each aligned block of 32 rows (0 to 31, 32 to 63, ..., all dimensions but the last counted through in order) at most 12 rows name the same one
- gate_weights: float32 [8, 128, 4], P('req'), may hold values from 0.1 to 0.7
- w_gate_up: bfloat16 [16, 2, 2880, 2880], P('req', None, None, 'kv'), may hold values from -0.109375 to 0.109375
- w_down: bfloat16 [16, 2880, 2880], P('req', 'kv'), may hold values from -0.109375 to 0.109375
Outputs:
- layer_out: bfloat16 [8, 128, 2880], P('req', 'kv')
Inputs may be any that keep to these rules, and one draw needn't show every extreme that they name: `routes`: each token names 4 different experts. In each aligned block of 32 tokens (requests first, then new tokens) no expert is named by more than 12 tokens, and some block reaches 12. `page_table`: each row names every one of its request's 128 pages once. `cache_lengths`: some request's cache is full.
All inputs are finite; a program needn't handle non-finite values.
Results may differ from a plain program's by a relative error of at most 0.014.
Values may be sent and summed in bfloat16 or wider, within the bound.
A program may use at most 192 MiB of HBM per device.

v0:
```python
import jax
import jax.numpy as jnp
from jax import lax
from jax.sharding import PartitionSpec as P

HD = 64
TOP = 4
GROUP = 8


THETA_BASE = 150000.0
EPSILON = 1e-05
ALPHA_GLU = 1.702


def rms_scale(row_data, gain_vector):
    row_data = row_data.astype(jnp.float32)
    mean_square = jnp.mean(row_data * row_data, axis=-1, keepdims=True)
    return row_data * lax.rsqrt(mean_square + EPSILON) * gain_vector


def rotate(vectors, positions):
    half_dim = vectors.shape[-1] // 2
    frequency = THETA_BASE ** (-(jnp.arange(half_dim, dtype=jnp.float32) * 2.0 / vectors.shape[-1]))
    angles = positions.astype(jnp.float32)[:, None] * frequency[None, :]
    view_shape = (vectors.shape[0],) + (1,) * (vectors.ndim - 2) + (half_dim,)
    cosine = jnp.cos(angles).reshape(view_shape)
    sine_part = jnp.sin(angles).reshape(view_shape)
    first_half = vectors[..., :half_dim]
    second_half = vectors[..., half_dim:]
    return jnp.concatenate(
        [
            first_half * cosine - second_half * sine_part,
            second_half * cosine + first_half * sine_part,
        ],
        axis=-1,
    )


def on_device(
    tokens,
    attn_gain,
    w_qkv,
    sink_logits,
    w_out,
    kv_cache,
    page_table,
    cache_lengths,
    moe_gain,
    routes,
    gate_weights,
    w_gate_up,
    w_down,
):
    kv_count = lax.axis_size("kv")
    req_count = lax.axis_size("req")
    place = lax.axis_index("kv")
    new_count = tokens.shape[1]
    model_width = tokens.shape[2]
    rows_dev = new_count // kv_count
    heads_dev = w_qkv.shape[1] // ((GROUP + 2) * HD)
    score_scale = HD ** (-0.5)
    page_size = kv_cache.shape[1]
    own_tokens = tokens[0]
    cached_length = cache_lengths[0]
    normed = rms_scale(own_tokens, attn_gain).astype(jnp.bfloat16)
    projected = jnp.dot(normed, w_qkv, preferred_element_type=jnp.float32).reshape(
        new_count, heads_dev, GROUP + 2, HD
    )
    positions = cached_length + jnp.arange(new_count, dtype=jnp.int32)
    queries = rotate(projected[:, :, :GROUP], positions).astype(jnp.bfloat16)
    new_keys = rotate(projected[:, :, GROUP], positions).astype(jnp.bfloat16)
    new_values = projected[:, :, GROUP + 1].astype(jnp.bfloat16)
    queries_wide = jnp.concatenate([queries, jnp.zeros_like(queries)], axis=-1).transpose(
        1, 2, 0, 3
    )
    new_block = jnp.concatenate([new_keys, new_values], axis=-1)
    sink_rows = sink_logits.reshape(heads_dev, GROUP)

    def absorb(carry_state, kv_block, visible):
        running_max, denominator, numerator = carry_state
        scores = (
            jnp.einsum("hgqd,khd->hgqk", queries_wide, kv_block, preferred_element_type=jnp.float32)
            * score_scale
        )
        block_peak = jnp.max(jnp.where(visible, scores, -jnp.inf), axis=-1)
        new_max = jnp.maximum(running_max, block_peak)
        weights = jnp.where(visible, jnp.exp(scores - new_max[..., None]), 0.0)
        factor = jnp.exp(running_max - new_max)
        denominator = denominator * factor + jnp.sum(weights, axis=-1)
        numerator = numerator * factor[..., None] + jnp.einsum(
            "hgqk,khd->hgqd",
            weights.astype(jnp.bfloat16),
            kv_block,
            preferred_element_type=jnp.float32,
        )
        return (new_max, denominator, numerator)

    init_state = (
        jnp.broadcast_to(sink_rows[:, :, None], (heads_dev, GROUP, new_count)),
        jnp.zeros((heads_dev, GROUP, new_count), jnp.float32),
        jnp.zeros((heads_dev, GROUP, new_count, 2 * HD), jnp.float32),
    )
    page_row = page_table[0]
    pages_block = min(8, page_table.shape[1])

    def cache_step(block_number, carry_state):
        for inner in range(pages_block):
            page_number = block_number * pages_block + inner
            page_id = lax.dynamic_index_in_dim(page_row, page_number, 0, False)
            page_data = lax.dynamic_index_in_dim(kv_cache, page_id, 0, False).reshape(
                page_size, heads_dev, 2 * HD
            )
            key_position = page_number * page_size + jnp.arange(page_size, dtype=jnp.int32)
            visible = (key_position < cached_length)[None, None, None, :]
            carry_state = absorb(carry_state, page_data, visible)
        return carry_state

    steps_count = page_table.shape[1] // pages_block
    carry_state = lax.fori_loop(0, steps_count, cache_step, init_state)
    query_position = jnp.arange(new_count, dtype=jnp.int32)
    causal = (query_position[None, :] <= query_position[:, None])[None, None]
    running_max, denominator, numerator = absorb(carry_state, new_block, causal)
    denominator = denominator + jnp.exp(sink_rows[:, :, None] - running_max)
    attended = (numerator[..., HD:] / denominator[..., None]).astype(jnp.bfloat16)
    attended = attended.transpose(2, 0, 1, 3).reshape(new_count, heads_dev * GROUP * HD)
    own_start = place * rows_dev
    partial_out = jnp.dot(attended, w_out, preferred_element_type=jnp.float32)
    summed_out = lax.psum(partial_out.astype(jnp.bfloat16), "kv").astype(jnp.float32)
    residual_all = own_tokens.astype(jnp.float32) + summed_out
    normed_all = rms_scale(residual_all, moe_gain).astype(jnp.bfloat16)
    residual = lax.dynamic_slice_in_dim(residual_all, own_start, rows_dev, 0)
    experts_dev = w_gate_up.shape[0]
    experts_all = experts_dev * req_count
    capacity = max(2, (6 * rows_dev + experts_all - 1) // experts_all)
    route_rows = routes[0]
    gate_rows = gate_weights[0]
    route_blocks = route_rows.reshape(kv_count, rows_dev * TOP)
    expert_hits = (
        route_blocks[:, :, None] == jnp.arange(experts_all, dtype=jnp.int32)[None, None, :]
    ).astype(jnp.int32)
    expert_rank = jnp.sum(jnp.cumsum(expert_hits, axis=1) * expert_hits, axis=2) - 1
    owner_block = jnp.arange(kv_count, dtype=jnp.int32)[:, None]
    slot_index = ((route_blocks * kv_count + owner_block) * capacity + expert_rank).reshape(
        new_count, TOP
    )
    buffer = jnp.zeros((experts_all * kv_count * capacity, model_width), jnp.bfloat16)
    buffer = buffer.at[slot_index.reshape(-1)].set(jnp.repeat(normed_all, TOP, axis=0))
    buffer = buffer.reshape(req_count, experts_dev, kv_count, capacity, model_width)
    arrived = lax.all_to_all(buffer, "req", split_axis=0, concat_axis=0, tiled=True)
    outputs = []
    for expert in range(experts_dev):
        expert_rows = arrived[:, expert]
        flat_rows = expert_rows.reshape(-1, model_width)
        gate_part = jnp.dot(flat_rows, w_gate_up[expert, 0], preferred_element_type=jnp.float32)
        up_part = jnp.dot(flat_rows, w_gate_up[expert, 1], preferred_element_type=jnp.float32)
        activated = (gate_part * jax.nn.sigmoid(ALPHA_GLU * gate_part) * (up_part + 1.0)).astype(
            jnp.bfloat16
        )
        expert_out = jnp.dot(activated, w_down[expert], preferred_element_type=jnp.float32)
        outputs.append(expert_out.reshape(expert_rows.shape))
    returned = lax.all_to_all(
        jnp.stack(outputs, axis=1).astype(jnp.bfloat16),
        "req",
        split_axis=0,
        concat_axis=0,
        tiled=True,
    ).astype(jnp.float32)
    flat_back = returned.reshape(experts_all * kv_count * capacity, model_width)
    gate_part = gate_rows
    picked = flat_back[slot_index]
    mixture = lax.psum_scatter(
        jnp.sum(gate_part[:, :, None] * picked, axis=1).astype(jnp.bfloat16),
        "kv",
        scatter_dimension=0,
        tiled=True,
    ).astype(jnp.float32)
    result = (residual + mixture).astype(jnp.bfloat16)
    return result[None]


def solution(mesh):
    in_specs = (
        P("req", None, None),
        P(),
        P(None, "kv"),
        P("kv"),
        P("kv", None),
        P("req", None, "kv"),
        P("req", None),
        P("req"),
        P(),
        P("req", None, None),
        P("req", None, None),
        P("req", None, None, "kv"),
        P("req", "kv", None),
    )
    out_specs = P("req", "kv", None)
    return jax.shard_map(
        on_device, mesh=mesh, in_specs=in_specs, out_specs=out_specs, check_vma=False
    )
```

profile of v0, /device:TPU:0, one launch (start us, length us, event | category | flops | bytes accessed | tf_op | source)
XLA Modules:
  0.0 1061.4 jit_solution(8598379459891960202)
XLA Ops:
  6.6 10.5 copy.143
  17.5 5.4 fusion.107
  26.1 11.9 %copy.144 = bf16[128,128,256]{1,2,0:T(8,128)(2,1)} copy(bf16[128,128,256]{2,1,0:T(8,128)(2,1)} %param.20) | data formatting | bytes 16777216
  38.2 612.8 %while.20 = (s32[]{:T(128)}, f32[2,8,128]{2,1,0:T(8,128)S(1)}, f32[2,8,128]{2,1,0:T(8,128)}, f32[2,8,128,128]{3,2,1,0:T(8,128)}, s32[]{:T(128)}, /*index=5*/s32[...) while((s32[]{:T(128)}, f32[2,8,128]{2,1,0:T(8,128)S(1)}, ...), condition=%wide.region_18.19_spmd.clone, body=%wide.region_1.18_spmd.clone.sunk | while | flops 1097109504 | bytes 95089504 | solution.py:120
  106.0 2.5 fusion.225
  144.3 2.5 fusion.225
  335.9 2.5 fusion.225
  653.5 5.3 convolution_convert_fusion.2
  659.8 36.0 %all-reduce.3.cloned.1.call-done = bf16[128,2880]{0,1:T(8,128)(2,1)} async-done(((bf16[128,2880]{0,1:T(8,128)(2,1)}), bf16[128,2880]{0,1:T(8,128)(2,1)}) %all-reduce.3.cloned.1.call-update) | async-done | bytes 737296 | tf_op jit(solution)/shard_map/psum | solution.py:129
  695.9 2.7 fusion.78
  702.0 2.9 reshape.481
  704.9 9.0 scatter_custom_fusion
  713.9 7.4 reshape.461
  721.2 4.5 copy.155
  725.7 105.8 %all_to_all.10 = bf16[8,2,4,12,2880]{4,2,3,1,0:T(4,128)(2,1)S(1)} all-to-all(bf16[8,2,4,12,2880]{4,2,3,1,0:T(4,128)(2,1)S(1)} %copy.155), channel_id=1, replica_groups=mesh['req'=8,'kv'=4] {'req'}, dimensions={0} | all-to-all | bytes 8847360 | tf_op jit(solution)/shard_map/all_to_all | solution.py:150
  831.5 2.6 fusion.130
  836.9 5.5 fusion.62
  842.4 4.8 fusion.98
  853.0 5.5 fusion.58
  858.5 4.8 fusion.95
  863.8 5.0 fusion.70
  868.8 5.4 fusion.73
  875.3 3.9 copy.160
  879.2 4.7 all-to-all-start.1
  884.5 98.5 %all-to-all-done.1 = bf16[8,2,4,12,2880]{4,2,3,1,0:T(4,128)(2,1)} async-done(((bf16[8,2,4,12,2880]{4,2,3,1,0:T(4,128)(2,1)}), bf16[8,2,4,12,2880]{4,2,3,1,0:T(4,128)(2,1)}, u32[]{:S(2)}, u32[]{:S(2)}) %all-to-all-start.1) | async-done | bytes 4423712 | tf_op jit(solution)/shard_map/all_to_all | solution.py:162
  983.0 3.7 copy_convert_fusion
  986.7 6.3 copy.162
  993.0 10.3 reshape.468
  1003.3 10.6 gather_fusion
  1013.9 7.6 reshape.470
  1021.5 7.1 multiply_reduce_fusion
  1030.2 21.5 %reduce-scatter.4.cloned.1.call-done = bf16[32,2880]{1,0:T(8,128)(2,1)} async-done(((bf16[128,2880]{1,0:T(8,128)(2,1)}), bf16[32,2880]{1,0:T(8,128)(2,1)}) %reduce-scatter.4.cloned.1.call-update) | async-done | bytes 184336
  (1429 shorter events, 382.7 us)
Async XLA Ops:
  6.5 689.3 %all-reduce.3.cloned.1.call-start = ((), (), s32[]{:S(2)}) async-start(), calls=%async_computation.3 | async-start | bytes 1474560 | tf_op jit(solution)/shard_map/psum | solution.py:129
  6.5 10.5 copy-start.12
  6.6 10.9 %copy-start.39 = (f32[2880]{0:T(1024)S(1)}, f32[2880]{0:T(1024)}, u32[]{:S(2)}) copy-start(f32[2880]{0:T(1024)} %param.16) | copy-start | bytes 34564
  26.1 12.0 %copy-start.41 = (f32[2,8]{1,0:T(2,128)}, f32[2,8]{1,0:T(2,128)S(1)}, u32[]{:S(2)}) copy-start(f32[2,8]{1,0:T(2,128)S(1)} %broadcast_in_dim.345) | copy-start | bytes 196
  26.1 12.0 %copy-start.18 = (s32[1,128]{1,0:T(1,128)S(1)}, s32[1,128]{1,0:T(1,128)}, u32[]{:S(2)}) copy-start(s32[1,128]{1,0:T(1,128)} %param.21) | copy-start | bytes 1540
  56.1 10.7 %copy-start.24 = (pred[128]{0:T(512)(128)(4,1)}, pred[128]{0:T(512)(128)(4,1)S(1)}, u32[]{:S(2)}) copy-start(pred[128]{0:T(512)(128)(4,1)S(1)} %get-tuple-element.478) | copy-start | bytes 388 | tf_op jit(solution)/shard_map/while
  93.4 10.7 %copy-start.24 = (pred[128]{0:T(512)(128)(4,1)}, pred[128]{0:T(512)(128)(4,1)S(1)}, u32[]{:S(2)}) copy-start(pred[128]{0:T(512)(128)(4,1)S(1)} %get-tuple-element.478) | copy-start | bytes 388 | tf_op jit(solution)/shard_map/while
  131.7 10.7 %copy-start.24 = (pred[128]{0:T(512)(128)(4,1)}, pred[128]{0:T(512)(128)(4,1)S(1)}, u32[]{:S(2)}) copy-start(pred[128]{0:T(512)(128)(4,1)S(1)} %get-tuple-element.478) | copy-start | bytes 388 | tf_op jit(solution)/shard_map/while
  170.0 10.7 %copy-start.24 = (pred[128]{0:T(512)(128)(4,1)}, pred[128]{0:T(512)(128)(4,1)S(1)}, u32[]{:S(2)}) copy-start(pred[128]{0:T(512)(128)(4,1)S(1)} %get-tuple-element.478) | copy-start | bytes 388 | tf_op jit(solution)/shard_map/while
  171.1 9.4 copy-start.26
  208.3 10.7 %copy-start.24 = (pred[128]{0:T(512)(128)(4,1)}, pred[128]{0:T(512)(128)(4,1)S(1)}, u32[]{:S(2)}) copy-start(pred[128]{0:T(512)(128)(4,1)S(1)} %get-tuple-element.478) | copy-start | bytes 388 | tf_op jit(solution)/shard_map/while
  209.4 9.4 copy-start.26
  246.7 10.7 %copy-start.24 = (pred[128]{0:T(512)(128)(4,1)}, pred[128]{0:T(512)(128)(4,1)S(1)}, u32[]{:S(2)}) copy-start(pred[128]{0:T(512)(128)(4,1)S(1)} %get-tuple-element.478) | copy-start | bytes 388 | tf_op jit(solution)/shard_map/while
  285.0 10.7 %copy-start.24 = (pred[128]{0:T(512)(128)(4,1)}, pred[128]{0:T(512)(128)(4,1)S(1)}, u32[]{:S(2)}) copy-start(pred[128]{0:T(512)(128)(4,1)S(1)} %get-tuple-element.478) | copy-start | bytes 388 | tf_op jit(solution)/shard_map/while
  286.0 9.4 copy-start.26
  323.3 10.7 %copy-start.24 = (pred[128]{0:T(512)(128)(4,1)}, pred[128]{0:T(512)(128)(4,1)S(1)}, u32[]{:S(2)}) copy-start(pred[128]{0:T(512)(128)(4,1)S(1)} %get-tuple-element.478) | copy-start | bytes 388 | tf_op jit(solution)/shard_map/while
  361.6 10.7 %copy-start.24 = (pred[128]{0:T(512)(128)(4,1)}, pred[128]{0:T(512)(128)(4,1)S(1)}, u32[]{:S(2)}) copy-start(pred[128]{0:T(512)(128)(4,1)S(1)} %get-tuple-element.478) | copy-start | bytes 388 | tf_op jit(solution)/shard_map/while
  362.7 9.4 copy-start.26
  399.9 10.7 %copy-start.24 = (pred[128]{0:T(512)(128)(4,1)}, pred[128]{0:T(512)(128)(4,1)S(1)}, u32[]{:S(2)}) copy-start(pred[128]{0:T(512)(128)(4,1)S(1)} %get-tuple-element.478) | copy-start | bytes 388 | tf_op jit(solution)/shard_map/while
  438.3 10.7 %copy-start.24 = (pred[128]{0:T(512)(128)(4,1)}, pred[128]{0:T(512)(128)(4,1)S(1)}, u32[]{:S(2)}) copy-start(pred[128]{0:T(512)(128)(4,1)S(1)} %get-tuple-element.478) | copy-start | bytes 388 | tf_op jit(solution)/shard_map/while
  476.6 10.7 %copy-start.24 = (pred[128]{0:T(512)(128)(4,1)}, pred[128]{0:T(512)(128)(4,1)S(1)}, u32[]{:S(2)}) copy-start(pred[128]{0:T(512)(128)(4,1)S(1)} %get-tuple-element.478) | copy-start | bytes 388 | tf_op jit(solution)/shard_map/while
  514.9 10.7 %copy-start.24 = (pred[128]{0:T(512)(128)(4,1)}, pred[128]{0:T(512)(128)(4,1)S(1)}, u32[]{:S(2)}) copy-start(pred[128]{0:T(512)(128)(4,1)S(1)} %get-tuple-element.478) | copy-start | bytes 388 | tf_op jit(solution)/shard_map/while
  553.2 10.7 %copy-start.24 = (pred[128]{0:T(512)(128)(4,1)}, pred[128]{0:T(512)(128)(4,1)S(1)}, u32[]{:S(2)}) copy-start(pred[128]{0:T(512)(128)(4,1)S(1)} %get-tuple-element.478) | copy-start | bytes 388 | tf_op jit(solution)/shard_map/while
  554.3 9.4 copy-start.26
  591.6 10.7 %copy-start.24 = (pred[128]{0:T(512)(128)(4,1)}, pred[128]{0:T(512)(128)(4,1)S(1)}, u32[]{:S(2)}) copy-start(pred[128]{0:T(512)(128)(4,1)S(1)} %get-tuple-element.478) | copy-start | bytes 388 | tf_op jit(solution)/shard_map/while
  629.9 10.7 %copy-start.24 = (pred[128]{0:T(512)(128)(4,1)}, pred[128]{0:T(512)(128)(4,1)S(1)}, u32[]{:S(2)}) copy-start(pred[128]{0:T(512)(128)(4,1)S(1)} %get-tuple-element.478) | copy-start | bytes 388 | tf_op jit(solution)/shard_map/while
  630.9 9.4 copy-start.26
  653.4 42.4 %copy-start.13 = (bf16[1,128,2880]{1,2,0:T(8,128)(2,1)S(1)}, bf16[1,128,2880]{1,2,0:T(8,128)(2,1)}, u32[]{:S(2)}) copy-start(bf16[1,128,2880]{1,2,0:T(8,128)(2,1)} %param.15) | copy-start | bytes 2211844
  658.8 39.8 %copy-start.40 = (f32[2880]{0:T(1024)S(1)}, f32[2880]{0:T(1024)}, u32[]{:S(2)}) copy-start(f32[2880]{0:T(1024)} %param.23) | copy-start | bytes 34564
  879.2 103.8 %all-to-all-start.1 = ((bf16[8,2,4,12,2880]{4,2,3,1,0:T(4,128)(2,1)}), bf16[8,2,4,12,2880]{4,2,3,1,0:T(4,128)(2,1)}, u32[]{:S(2)}, u32[]{:S(2)}) async-start(bf16[8,2,4,12,2880]{4,2,3,1,0:T(4,128)(2,1)} %copy.160), calls=%async_computation.1 | async-start | bytes 9043968 | tf_op jit(solution)/shard_map/all_to_all | solution.py:162
  883.9 167.8 %reduce-scatter.4.cloned.1.call-start = ((), (), s32[]{:S(2)}) async-start(), calls=%async_computation.4 | async-start | bytes 942080
  1028.6 24.4 %copy-start.14 = (f32[128,2880]{0,1:T(8,128)S(1)}, f32[128,2880]{0,1:T(8,128)}, u32[]{:S(2)}) copy-start(f32[128,2880]{0,1:T(8,128)} %get-tuple-element.351) | copy-start | bytes 4423684
  (392 other events, 1248.1 us)
Sparse Core Ops, SparseCore 0:
  658.9 36.8 all-reduce.2
  1030.3 21.3 reduce-scatter.3
where the time goes:
time: 1070 us; the launch traced here: 1060 us
  matrix products  267 us (25%)
  loops' own time  247 us (23%)
  local copies, waits for them, and re-layouts  156 us (15%)
  waiting for transfers between devices  156 us (15%)
  other arithmetic  111 us (10%)
  blocking collectives  106 us (10%)
  between operations  14.8 us (1%)
    another operation x1, loops' own time, on_device(): carry_state = lax.fori_loop(0, steps_count, cache_step, init_state)  247 us
    dot_general x129, matrix products, absorb(): jnp.einsum('hgqk,khd->hgqd', weights.astype(jnp.bfloat16), kv_block, pref...  129 us
    all_to_all x1, blocking collectives, on_device(): lax.all_to_all(buffer, 'req', split_axis=0, concat_axis=0, tiled=True)  106 us
    all_to_all x1, waiting for transfers between devices, on_device(): lax.all_to_all(jnp.stack(outputs, axis=1).astype(jnp.bfloat16), 'req', sp...  98.5 us
    dot_general x129, matrix products, absorb(): jnp.einsum('hgqd,khd->hgqk', queries_wide, kv_block, preferred_element_ty...  95.5 us
    lt x64, other arithmetic, cache_step(): visible = (key_position < cached_length)[None, None, None, :]  41.7 us
    psum x1, waiting for transfers between devices, on_device(): lax.psum(partial_out.astype(jnp.bfloat16), 'kv').astype(jnp.float32)  36 us
    reduce_sum x129, other arithmetic, absorb(): denominator = denominator * factor + jnp.sum(weights, axis=-1)  28.3 us
  transfers between devices with their start and end apart: 3, of which 3 were waited for; matrix products, arithmetic and copies ran while one was open for 0% of the time, Pallas kernels for 0%

commit v1 on v0

v1 whole, which is shorter than its diff:
```python
import functools

import jax
import jax.numpy as jnp
from jax import lax
from jax.experimental import pallas as pl
from jax.experimental.pallas import tpu as pltpu
from jax.sharding import PartitionSpec as P

HD = 64
TOP = 4
GROUP = 8


THETA_BASE = 150000.0
EPSILON = 1e-05
ALPHA_GLU = 1.702


def rms_scale(row_data, gain_vector):
    row_data = row_data.astype(jnp.float32)
    mean_square = jnp.mean(row_data * row_data, axis=-1, keepdims=True)
    return row_data * lax.rsqrt(mean_square + EPSILON) * gain_vector


def rotate(vectors, positions):
    half_dim = vectors.shape[-1] // 2
    frequency = THETA_BASE ** (-(jnp.arange(half_dim, dtype=jnp.float32) * 2.0 / vectors.shape[-1]))
    angles = positions.astype(jnp.float32)[:, None] * frequency[None, :]
    view_shape = (vectors.shape[0],) + (1,) * (vectors.ndim - 2) + (half_dim,)
    cosine = jnp.cos(angles).reshape(view_shape)
    sine_part = jnp.sin(angles).reshape(view_shape)
    first_half = vectors[..., :half_dim]
    second_half = vectors[..., half_dim:]
    return jnp.concatenate(
        [
            first_half * cosine - second_half * sine_part,
            second_half * cosine + first_half * sine_part,
        ],
        axis=-1,
    )


QUERY_CHUNK = 256


def attention_kernel(
    pages_ref, length_ref, query_ref, fresh_ref, sink_ref, *rest, new_count, page_size, page_step
):
    page_refs = rest[:page_step]
    out_ref, peak_ref, total_ref = rest[page_step:]
    heads, width, columns = query_ref.shape
    step = pl.program_id(0)
    length = length_ref[0]
    span = page_step * page_size
    chunk = min(QUERY_CHUNK, columns)

    def value_side(block):
        lane = lax.broadcasted_iota(jnp.int32, block.shape, 1)
        return jnp.where(lane < HD, jnp.ones_like(block), block)

    def weighted(block, weights):
        return lax.dot_general(
            block, weights, (((0,), (0,)), ((), ())), preferred_element_type=jnp.float32
        )

    @pl.when(step == 0)
    def _():
        key_at = lax.broadcasted_iota(jnp.int32, (new_count, columns), 0)
        query_at = lax.broadcasted_iota(jnp.int32, (new_count, columns), 1) % new_count
        causal = key_at <= query_at
        for head in range(heads):
            block = fresh_ref[:, head * width : (head + 1) * width]
            scores = jnp.dot(block, query_ref[head], preferred_element_type=jnp.float32)
            scores = jnp.where(causal, scores, -jnp.inf)
            sink = sink_ref[head : head + 1, :]
            peak = jnp.maximum(sink, jnp.max(scores, axis=0, keepdims=True))
            weights = jnp.exp(scores - peak).astype(jnp.bfloat16)
            row = lax.broadcasted_iota(jnp.int32, (width, columns), 0)
            start = jnp.where(row < HD, jnp.exp(sink - peak), 0.0)
            total_ref[head] = start + weighted(value_side(block), weights)
            peak_ref[head : head + 1, :] = peak

    def absorb(masked):
        for head in range(heads):
            block = jnp.concatenate(
                [page[0, :, head * width : (head + 1) * width] for page in page_refs], axis=0
            )
            value_block = value_side(block)
            for at in range(0, columns, chunk):
                part = slice(at, at + chunk)
                scores = jnp.dot(
                    block, query_ref[head, :, part], preferred_element_type=jnp.float32
                )
                if masked:
                    key_at = step * span + lax.broadcasted_iota(jnp.int32, scores.shape, 0)
                    scores = jnp.where(key_at < length, scores, -jnp.inf)
                old_peak = peak_ref[head : head + 1, part]
                peak = jnp.maximum(old_peak, jnp.max(scores, axis=0, keepdims=True))
                weights = jnp.exp(scores - peak).astype(jnp.bfloat16)
                total_ref[head, :, part] = total_ref[head, :, part] * jnp.exp(
                    old_peak - peak
                ) + weighted(value_block, weights)
                peak_ref[head : head + 1, part] = peak

    @pl.when((step + 1) * span <= length)
    def _():
        absorb(False)

    @pl.when(((step + 1) * span > length) & (step * span < length))
    def _():
        absorb(True)

    @pl.when(step == pl.num_programs(0) - 1)
    def _():
        for head in range(heads):
            total = total_ref[head]
            out_ref[head] = (total[HD:] / total[0:1]).astype(jnp.bfloat16)


def cache_attention(queries, new_block, sink_rows, kv_cache, page_row, cached_length):
    new_count, heads, group, _ = queries.shape
    page_size, cache_width = kv_cache.shape[1:]
    columns = group * new_count
    page_step = 8
    while page_row.shape[0] % page_step:
        page_step //= 2
    turned = (queries * jnp.bfloat16(HD**-0.5)).transpose(1, 3, 2, 0).reshape(heads, HD, columns)
    turned = jnp.concatenate([turned, jnp.zeros_like(turned)], axis=1)
    sink_columns = jnp.repeat(sink_rows, new_count, axis=1)
    fixed = lambda rank: (lambda step, pages, length: (0,) * rank)

    def page_spec(place):
        return pl.BlockSpec(
            (1, page_size, cache_width),
            lambda step, pages, length: (pages[step * page_step + place], 0, 0),
        )

    out = pl.pallas_call(
        functools.partial(
            attention_kernel, new_count=new_count, page_size=page_size, page_step=page_step
        ),
        grid_spec=pltpu.PrefetchScalarGridSpec(
            num_scalar_prefetch=2,
            grid=(page_row.shape[0] // page_step,),
            in_specs=[
                pl.BlockSpec((heads, 2 * HD, columns), fixed(3)),
                pl.BlockSpec((new_count, cache_width), fixed(2)),
                pl.BlockSpec((heads, columns), fixed(2)),
            ]
            + [page_spec(place) for place in range(page_step)],
            out_specs=pl.BlockSpec((heads, HD, columns), fixed(3)),
            scratch_shapes=[
                pltpu.VMEM((heads, columns), jnp.float32),
                pltpu.VMEM((heads, 2 * HD, columns), jnp.float32),
            ],
        ),
        out_shape=jax.ShapeDtypeStruct((heads, HD, columns), jnp.bfloat16),
        compiler_params=pltpu.CompilerParams(vmem_limit_bytes=40 * 1024 * 1024),
        name="cache_attention",
    )(page_row, cached_length, turned, new_block, sink_columns, *([kv_cache] * page_step))
    out = out.reshape(heads, HD, group, new_count).transpose(3, 0, 2, 1)
    return out.reshape(new_count, heads * group * HD)


def on_device(
    tokens,
    attn_gain,
    w_qkv,
    sink_logits,
    w_out,
    kv_cache,
    page_table,
    cache_lengths,
    moe_gain,
    routes,
    gate_weights,
    w_gate_up,
    w_down,
):
    kv_count = lax.axis_size("kv")
    req_count = lax.axis_size("req")
    place = lax.axis_index("kv")
    new_count = tokens.shape[1]
    rows_dev = new_count // kv_count
    heads_dev = w_qkv.shape[1] // ((GROUP + 2) * HD)
    own_tokens = tokens[0]
    experts_dev = w_gate_up.shape[0]
    experts_all = experts_dev * req_count
    hidden_dev = w_down.shape[1]

    chosen = routes[0][:, :, None] == jnp.arange(experts_all, dtype=jnp.int32)
    expert_gates = jnp.sum(jnp.where(chosen, gate_weights[0][:, :, None], 0.0), axis=1)
    all_gates = lax.all_gather(expert_gates, "req", axis=0, tiled=True)
    own_gates = lax.dynamic_slice_in_dim(
        all_gates, lax.axis_index("req") * experts_dev, experts_dev, 1
    )

    normed = rms_scale(own_tokens, attn_gain).astype(jnp.bfloat16)
    projected = jnp.dot(normed, w_qkv, preferred_element_type=jnp.float32).reshape(
        new_count, heads_dev, GROUP + 2, HD
    )
    positions = cache_lengths[0] + jnp.arange(new_count, dtype=jnp.int32)
    queries = rotate(projected[:, :, :GROUP], positions).astype(jnp.bfloat16)
    new_keys = rotate(projected[:, :, GROUP], positions).astype(jnp.bfloat16)
    new_values = projected[:, :, GROUP + 1].astype(jnp.bfloat16)
    new_block = jnp.concatenate([new_keys, new_values], axis=-1).reshape(new_count, -1)
    attended = cache_attention(
        queries,
        new_block,
        sink_logits.reshape(heads_dev, GROUP),
        kv_cache,
        page_table[0],
        cache_lengths,
    )

    partial_out = jnp.dot(attended, w_out, preferred_element_type=jnp.float32)
    summed_out = lax.psum_scatter(
        partial_out.astype(jnp.bfloat16), "kv", scatter_dimension=0, tiled=True
    ).astype(jnp.float32)
    own_rows = lax.dynamic_slice_in_dim(own_tokens, place * rows_dev, rows_dev, 0)
    residual = own_rows.astype(jnp.float32) + summed_out
    moe_rows = rms_scale(residual, moe_gain).astype(jnp.bfloat16)
    moe_in = lax.all_gather(moe_rows, ("req", "kv"), axis=0, tiled=True)
    hidden = []
    for expert in range(experts_dev):
        gate_part = jnp.dot(moe_in, w_gate_up[expert, 0], preferred_element_type=jnp.float32)
        up_part = jnp.dot(moe_in, w_gate_up[expert, 1], preferred_element_type=jnp.float32)
        activated = gate_part * jax.nn.sigmoid(ALPHA_GLU * gate_part) * (up_part + 1.0)
        hidden.append((activated * own_gates[:, expert : expert + 1]).astype(jnp.bfloat16))
    mixed_part = jnp.dot(
        jnp.concatenate(hidden, axis=1),
        w_down.reshape(experts_dev * hidden_dev, -1),
        preferred_element_type=jnp.float32,
    ).astype(jnp.bfloat16)
    mixture = lax.psum_scatter(
        mixed_part, ("req", "kv"), scatter_dimension=0, tiled=True
    ).astype(jnp.float32)
    return (residual + mixture).astype(jnp.bfloat16)[None]


def solution(mesh):
    in_specs = (
        P("req", None, None),
        P(),
        P(None, "kv"),
        P("kv"),
        P("kv", None),
        P("req", None, "kv"),
        P("req", None),
        P("req"),
        P(),
        P("req", None, None),
        P("req", None, None),
        P("req", None, None, "kv"),
        P("req", "kv", None),
    )
    out_specs = P("req", "kv", None)
    return jax.shard_map(
        on_device, mesh=mesh, in_specs=in_specs, out_specs=out_specs, check_vma=False
    )
```

time: 1070 us -> 421 us (0.39)
  loops' own time: 247 us -> 0 us
  matrix products: 267 us -> 56.8 us
  local copies, waits for them, and re-layouts: 156 us -> 14.9 us
  other arithmetic: 111 us -> 6.31 us
  waiting for transfers between devices: 156 us -> 244 us
  blocking collectives: 106 us -> 30.8 us
  Pallas kernels: 0 us -> 53.3 us
    another operation x1 -> x0, loops' own time: 247 us -> none  [on_device(): carry_state = lax.fori_loop(0, steps_count, cache_step, init_state)]
    dot_general x264 -> x5, matrix products: 256 us -> 45.6 us  [the longest x2 17.3 us: on_device(): jnp.dot(moe_in, w_gate_up[expert, 1], preferred_element_type=jnp.float32)]
    reduce_scatter x0 -> x2, waiting for transfers between devices: none -> 207 us  [the longest x1 143 us: on_device(): lax.psum_scatter(mixed_part, ('req', 'kv'), scatter_dimension=0, tiled=True)]
    all_to_all x1 -> x0, blocking collectives: 106 us -> none  [on_device(): lax.all_to_all(buffer, 'req', split_axis=0, concat_axis=0, tiled=True)]
    all_to_all x1 -> x0, waiting for transfers between devices: 98.5 us -> none  [on_device(): lax.all_to_all(jnp.stack(outputs, axis=1).astype(jnp.bfloat16), 'req', sp...]
    pallas_call x0 -> x1, Pallas kernels: none -> 53.3 us  [cache_attention(): pl.pallas_call(functools.partial(attention_kernel, new_count=new_count, p...]
    lt x64 -> x0, other arithmetic: 41.7 us -> none  [cache_step(): visible = (key_position < cached_length)[None, None, None, :]]
    all_gather x0 -> x1, waiting for transfers between devices: none -> 37.7 us  [on_device(): moe_in = lax.all_gather(moe_rows, ('req', 'kv'), axis=0, tiled=True)]
where the time goes in v1:
time: 421 us
  waiting for transfers between devices  244 us (58%)
  matrix products  56.8 us (13%)
  Pallas kernels  53.3 us (13%)
  blocking collectives  30.8 us (7%)
  local copies, waits for them, and re-layouts  14.9 us (4%)
  between operations  14 us (3%)
  other arithmetic  6.31 us (1%)
    reduce_scatter x1, waiting for transfers between devices, on_device(): lax.psum_scatter(mixed_part, ('req', 'kv'), scatter_dimension=0, tiled=True)  143 us
    reduce_scatter x1, waiting for transfers between devices, on_device(): lax.psum_scatter(partial_out.astype(jnp.bfloat16), 'kv', scatter_dimensio...  63.2 us
    pallas_call x1, Pallas kernels, cache_attention(): pl.pallas_call(functools.partial(attention_kernel, new_count=new_count, p...  53.3 us
    all_gather x1, waiting for transfers between devices, on_device(): moe_in = lax.all_gather(moe_rows, ('req', 'kv'), axis=0, tiled=True)  37.7 us
    all_gather x1, blocking collectives, on_device(): all_gates = lax.all_gather(expert_gates, 'req', axis=0, tiled=True)  30.8 us
    dot_general x2, matrix products, on_device(): jnp.dot(moe_in, w_gate_up[expert, 1], preferred_element_type=jnp.float32)  17.3 us
    dot_general x1, matrix products, on_device(): jnp.dot(jnp.concatenate(hidden, axis=1), w_down.reshape(experts_dev * hid...  14.7 us
    unnamed x34, local copies, waits for them, and re-layouts  14.3 us
  transfers between devices with their start and end apart: 3, of which 3 were waited for; matrix products, arithmetic and copies ran while one was open for 0% of the time, Pallas kernels for 0%

profile of v1, /device:TPU:0, one launch (start us, length us, event | category | flops | bytes accessed | tf_op | source)
XLA Modules:
  0.0 420.5 jit_solution(11416367167980609825)
XLA Ops:
  6.5 1.5 fusion.19
  8.1 0.0 copy-start.4
  8.1 10.5 %copy.30 = bf16[2880,1280]{0,1:T(8,128)(2,1)} copy(bf16[2880,1280]{1,0:T(8,128)(2,1)} %param.15) | data formatting | bytes 14745600 | tf_op args[2]
  18.6 5.4 %fusion.23 = f32[128,2,10,64]{0,3,2,1:T(8,128)S(1)} fusion(bf16[2,10,64,2880]{3,2,1,0:T(8,128)(2,1)} %bitcast.77, bf16[1,128,2880]{1,2,0:T(8,128)(2,1)S(1)} %copy-done.2, f32[2880]{0:T(1024)S(1)} %copy-done.4, f32[128]{0:T(128)S(1)} %add_rsqrt_fusion.1), kind=kOutput, calls=%fused_computation.25 | convolution fusion | flops 945192960 | bytes 8777472 | tf_op jit(solution)/shard_map/dot_general | solution.py:200
  24.8 0.1 reshape.174
  24.8 0.1 broadcast_bitcast_fusion
  24.9 0.1 multiply_cosine_fusion
  25.1 0.1 subtract_convert_fusion
  25.2 0.1 copy.36.fresh_ref
  25.4 3.4 copy-done
  28.8 53.3 %cache_attention.1 = bf16[2,64,1024]{2,1,0:T(8,128)(2,1)S(1)} custom-call(s32[128]{0:T(128)S(1)} %bitcast.76, s32[1]{0:T(128)} %copy.46.length_ref, bf16[2,128,1024]{2,1,0:T(8,128)(2,1)S(1)} %concatenate.17.query_ref, bf16[128,256]{1,0:T(8,128)(2,1)S(1)} %copy.36.fresh_ref, f32[2,1024]{1,0:T(2,128)S(1)} %bitcast.75, bf16[128,128,256]{2,1,0:T(8,128)(2,1)S(1)} %copy-done, ...), custom_call_target="tpu_custom_call" | custom-call | tf_op jit(solution)/shard_map/cache_attention/pallas_call | solution.py:139
  82.1 0.1 copy_bitcast_fusion.1
  82.2 5.7 %convolution_convert_fusion.1 = bf16[128,2880]{1,0:T(8,128)(2,1)} fusion(bf16[128,1024]{0,1:T(8,128)(2,1)S(1)} %bitcast.78, bf16[1024,2880]{0,1:T(8,128)(2,1)} %param.17), kind=kOutput, calls=%fused_computation.13 | convolution fusion | flops 755343360 | bytes 6897664 | tf_op jit(solution)/shard_map/dot_general | solution.py:217
  87.9 0.0 reduce-scatter.3.cloned.1.call-update
  87.9 0.0 all-gather.2.cloned.1.call-start
  88.0 0.3 constant_dynamic-slice_fusion.2
  88.3 0.3 copy.37
  88.5 63.2 %reduce-scatter.3.cloned.1.call-done = bf16[32,2880]{1,0:T(8,128)(2,1)} async-done(((bf16[128,2880]{1,0:T(8,128)(2,1)}), bf16[32,2880]{1,0:T(8,128)(2,1)}) %reduce-scatter.3.cloned.1.call-update) | async-done | bytes 184336 | tf_op jit(solution)/shard_map/reduce_scatter | solution.py:218
  151.8 1.1 multiply_reduce_fusion
  152.9 1.7 multiply_convert_fusion.2
  154.6 0.0 all-gather.2.cloned.1.call-update
  154.6 0.0 reduce-scatter.5.cloned.1.call-start
  154.7 30.8 %all_gather.7 = f32[1024,16]{0,1:T(8,128)S(1)} all-gather(f32[128,16]{0,1:T(8,128)S(1)} %select_reduce_fusion), channel_id=1, replica_groups=mesh['req'=8,'kv'=4] {'req'}, dimensions={0}, use_global_device_ids=true | all-gather | bytes 73728 | tf_op jit(solution)/shard_map/all_gather | solution.py:194
  185.5 37.7 %all-gather.2.cloned.1.call-done = bf16[1024,2880]{1,0:T(8,128)(2,1)} async-done(((bf16[32,2880]{1,0:T(8,128)(2,1)}), bf16[1024,2880]{1,0:T(8,128)(2,1)}) %all-gather.2.cloned.1.call-update) | async-done | bytes 5898256 | tf_op jit(solution)/shard_map/all_gather | solution.py:224
  223.2 10.5 %fusion = f32[1024,720]{0,1:T(8,128)} fusion(bf16[1024,2880]{1,0:T(8,128)(2,1)} %all-gather.2.cloned.1.call-done, bf16[2,2,2880,720]{2,3,1,0:T(8,128)(2,1)} %param.24), kind=kOutput, calls=%fused_computation.1 | convolution fusion | flops 4246732800 | bytes 13217792 | tf_op jit(solution)/shard_map/dot_general | solution.py:228
  233.7 6.8 %fusion.4 = f32[1024,720]{0,1:T(8,128)S(1)} fusion(bf16[1024,2880]{1,0:T(8,128)(2,1)S(1)} %copy-done.8, bf16[2,2,2880,720]{2,3,1,0:T(8,128)(2,1)} %param.24), kind=kOutput, calls=%fused_computation.5 | convolution fusion | flops 4246732800 | bytes 13086720 | tf_op jit(solution)/shard_map/dot_general | solution.py:228
  240.5 7.0 %multiply_convert_fusion = bf16[1024,720]{0,1:T(8,128)(2,1)S(1)} fusion(f32[1024,720]{0,1:T(8,128)} %fusion, bf16[1024,2880]{1,0:T(8,128)(2,1)S(1)} %copy-done.8, bf16[2,2,2880,720]{2,3,1,0:T(8,128)(2,1)S(1)} %bitcast.85, f32[1024]{0:T(1024)S(1)} %bitcast.81), kind=kOutput, calls=%fused_computation.17 | convolution fusion | flops 4253368320 | bytes 14696448 | tf_op jit(solution)/shard_map/dot_general | solution.py:227
  247.6 6.5 %multiply_convert_fusion.1 = bf16[1024,720]{0,1:T(8,128)(2,1)} fusion(f32[1024,720]{0,1:T(8,128)S(1)} %fusion.4, bf16[1024,2880]{1,0:T(8,128)(2,1)S(1)} %copy-done.8, bf16[2,2,2880,720]{2,3,1,0:T(8,128)(2,1)S(1)} %bitcast.85, f32[1024]{0:T(1024)S(1)} %bitcast.80), kind=kOutput, calls=%fused_computation.18 | convolution fusion | flops 4253368320 | bytes 14696448 | tf_op jit(solution)/shard_map/dot_general | solution.py:227
  254.1 14.7 %convolution_convert_fusion = bf16[1024,2880]{1,0:T(8,128)(2,1)} fusion(bf16[1440,2880]{1,0:T(8,128)(2,1)} %bitcast.86, bf16[1024,720]{0,1:T(8,128)(2,1)S(1)} %multiply_convert_fusion, bf16[1024,720]{0,1:T(8,128)(2,1)} %multiply_convert_fusion.1), kind=kOutput, calls=%fused_computation | convolution fusion | flops 8502312960 | bytes 17141760 | tf_op jit(solution)/shard_map/dot_general | solution.py:231
  268.8 0.0 reduce-scatter.5.cloned.1.call-update
  268.9 143.5 %reduce-scatter.5.cloned.1.call-done = bf16[32,2880]{1,0:T(8,128)(2,1)} async-done(((bf16[1024,2880]{1,0:T(8,128)(2,1)}), bf16[32,2880]{1,0:T(8,128)(2,1)}) %reduce-scatter.5.cloned.1.call-update) | async-done | bytes 184336 | tf_op jit(solution)/shard_map/reduce_scatter | solution.py:236
  412.3 1.7 fusion.28
  (43 shorter events, 0.2 us)
Async XLA Ops:
  6.5 145.2 %reduce-scatter.3.cloned.1.call-start = ((), (), s32[]{:S(2)}) async-start(), calls=%async_computation.2 | async-start | bytes 942080 | tf_op jit(solution)/shard_map/reduce_scatter | solution.py:218
  8.1 10.5 %copy-start.2 = (bf16[1,128,2880]{1,2,0:T(8,128)(2,1)S(1)}, bf16[1,128,2880]{1,2,0:T(8,128)(2,1)}, u32[]{:S(2)}) copy-start(bf16[1,128,2880]{1,2,0:T(8,128)(2,1)} %param.13) | copy-start | bytes 2211844
  8.1 10.5 %copy-start.4 = (f32[2880]{0:T(1024)S(1)}, f32[2880]{0:T(1024)}, u32[]{:S(2)}) copy-start(f32[2880]{0:T(1024)} %param.14) | copy-start | bytes 34564
  18.6 6.1 %copy-start.9 = (f32[16]{0:T(128)S(1)}, f32[16]{0:T(128)}, u32[]{:S(2)}) copy-start(f32[16]{0:T(128)} %param.16) | copy-start | bytes 196
  18.6 6.8 %copy-start.1 = (s32[1,128]{1,0:T(1,128)S(1)}, s32[1,128]{1,0:T(1,128)}, u32[]{:S(2)}) copy-start(s32[1,128]{1,0:T(1,128)} %param.19) | copy-start | bytes 1540
  25.4 3.4 copy-start
  87.9 65.0 %copy-start.5 = (f32[2880]{0:T(1024)S(1)}, f32[2880]{0:T(1024)}, u32[]{:S(2)}) copy-start(f32[2880]{0:T(1024)} %param.21) | copy-start | bytes 34564
  87.9 66.8 %copy-start.6 = (f32[1,128,4]{1,2,0:T(4,128)S(1)}, f32[1,128,4]{1,2,0:T(4,128)}, u32[]{:S(2)}) copy-start(f32[1,128,4]{1,2,0:T(4,128)} %param.23) | copy-start | bytes 6148
  87.9 66.8 %copy-start.7 = (s32[1,128,4]{1,2,0:T(4,128)S(1)}, s32[1,128,4]{1,2,0:T(4,128)}, u32[]{:S(2)}) copy-start(s32[1,128,4]{1,2,0:T(4,128)} %param.22) | copy-start | bytes 6148
  87.9 135.2 %all-gather.2.cloned.1.call-start = ((), (), s32[]{:S(2)}) async-start(), calls=%async_computation.3 | async-start | bytes 6217728 | tf_op jit(solution)/shard_map/all_gather | solution.py:224
  154.6 257.7 %reduce-scatter.5.cloned.1.call-start = ((), (), s32[]{:S(2)}) async-start(), calls=%async_computation.4 | async-start | bytes 6217728 | tf_op jit(solution)/shard_map/reduce_scatter | solution.py:236
  223.1 10.5 %copy-start.8 = (bf16[1024,2880]{1,0:T(8,128)(2,1)S(1)}, bf16[1024,2880]{1,0:T(8,128)(2,1)}, u32[]{:S(2)}) copy-start(bf16[1024,2880]{1,0:T(8,128)(2,1)} %all-gather.2.cloned.1.call-done) | copy-start | bytes 17694724
  223.1 17.3 %slice-start = ((s8[16957440]{0:T(1024)(128)(4,1)}), s8[4194304]{0:T(1024)(128)(4,1)S(1)}, s32[]{:S(2)}) async-start(s8[16957440]{0:T(1024)(128)(4,1)} %bitcast.84), calls=%async_computation.5 | async-start | bytes 8388608
  223.1 17.3 %slice-start.1 = ((s8[16957440]{0:T(1024)(128)(4,1)}), s8[4194304]{0:T(1024)(128)(4,1)S(1)}, s32[]{:S(2)}) async-start(s8[16957440]{0:T(1024)(128)(4,1)} %bitcast.84), calls=%async_computation.6 | async-start | bytes 8388608
  223.2 17.4 %slice-start.2 = ((s8[16957440]{0:T(1024)(128)(4,1)}), s8[4194304]{0:T(1024)(128)(4,1)S(1)}, s32[]{:S(2)}) async-start(s8[16957440]{0:T(1024)(128)(4,1)} %bitcast.84), calls=%async_computation.7 | async-start | bytes 8388608
  233.7 6.9 %slice-start.3 = ((s8[16957440]{0:T(1024)(128)(4,1)}), s8[4194304]{0:T(1024)(128)(4,1)S(1)}, s32[]{:S(2)}) async-start(s8[16957440]{0:T(1024)(128)(4,1)} %bitcast.84), calls=%async_computation.8 | async-start | bytes 8388608
  233.7 6.9 %slice-start.4 = ((s8[16957440]{0:T(1024)(128)(4,1)}), s8[180224]{0:T(1024)(128)(4,1)S(1)}, s32[]{:S(2)}) async-start(s8[16957440]{0:T(1024)(128)(4,1)} %bitcast.84), calls=%async_computation.9 | async-start | bytes 360448
  268.8 143.5 %copy-start.3 = (bf16[32,2880]{1,0:T(8,128)(2,1)S(1)}, bf16[32,2880]{1,0:T(8,128)(2,1)}, u32[]{:S(2)}) copy-start(bf16[32,2880]{1,0:T(8,128)(2,1)} %reduce-scatter.3.cloned.1.call-done) | copy-start | bytes 552964
Sparse Core Ops, SparseCore 0:
  88.1 63.6 reduce-scatter.2
  155.0 68.0 all-gather.1
  269.0 143.2 reduce-scatter.4

commit v2 on v1

--- a/solution.py
+++ b/solution.py
@@ -233,9 +233,11 @@
         w_down.reshape(experts_dev * hidden_dev, -1),
         preferred_element_type=jnp.float32,
     ).astype(jnp.bfloat16)
-    mixture = lax.psum_scatter(
-        mixed_part, ("req", "kv"), scatter_dimension=0, tiled=True
-    ).astype(jnp.float32)
+    parts = mixed_part.reshape(req_count, kv_count, rows_dev, -1).transpose(1, 0, 2, 3)
+    parts = lax.all_to_all(parts, "kv", split_axis=0, concat_axis=0, tiled=True)
+    hidden_sum = jnp.sum(parts.astype(jnp.float32), axis=0).astype(jnp.bfloat16)
+    expert_parts = lax.all_to_all(hidden_sum, "req", split_axis=0, concat_axis=0, tiled=True)
+    mixture = jnp.sum(expert_parts.astype(jnp.float32), axis=0)
     return (residual + mixture).astype(jnp.bfloat16)[None]
 
 

time: 421 us -> 412 us (0.979)
  waiting for transfers between devices: 244 us -> 67.6 us
  blocking collectives: 30.8 us -> 142 us
  Pallas kernels: 53.3 us -> 87.8 us
  local copies, waits for them, and re-layouts: 14.9 us -> 26.7 us
  matrix products: 56.8 us -> 64.1 us
    reduce_scatter x1 -> x0, waiting for transfers between devices: 143 us -> none  [on_device(): lax.psum_scatter(mixed_part, ('req', 'kv'), scatter_dimension=0, tiled=True)]
    all_to_all x0 -> x2, blocking collectives: none -> 111 us  [the longest x1 71.4 us: on_device(): parts = lax.all_to_all(parts, 'kv', split_axis=0, concat_axis=0, tiled=True)]
    pallas_call x1, Pallas kernels: 53.3 us -> 87.8 us  [cache_attention(): pl.pallas_call(functools.partial(attention_kernel, new_count=new_count, p...]
    reduce_scatter x1, waiting for transfers between devices: 63.2 us -> 29.8 us  [on_device(): lax.psum_scatter(partial_out.astype(jnp.bfloat16), 'kv', scatter_dimensio...]
    convert_element_type x0 -> x1, local copies, waits for them, and re-layouts: none -> 8.52 us  [on_device(): mixed_part = jnp.dot(jnp.concatenate(hidden, axis=1), w_down.reshape(expe...]
    dot_general x1, matrix products: 14.7 us -> 19.4 us  [on_device(): jnp.dot(jnp.concatenate(hidden, axis=1), w_down.reshape(experts_dev * hid...]
    reduce_sum x0 -> x2, other arithmetic: none -> 4.4 us  [the longest x1 4.2 us: on_device(): hidden_sum = jnp.sum(parts.astype(jnp.float32), axis=0).astype(jnp.bfloat16)]
  transfers between devices with their start and end apart: 3 -> 2, of which waited for: 3 -> 2; matrix products, arithmetic and copies ran while one was open for 0% -> 0% of each run, Pallas kernels for 0% -> 0%
where the time goes in v2:
time: 412 us
  blocking collectives  142 us (34%)
  Pallas kernels  87.8 us (21%)
  waiting for transfers between devices  67.6 us (16%)
  matrix products  64.1 us (16%)
  local copies, waits for them, and re-layouts  26.7 us (6%)
  between operations  14.3 us (3%)
  other arithmetic  9.79 us (2%)
    pallas_call x1, Pallas kernels, cache_attention(): pl.pallas_call(functools.partial(attention_kernel, new_count=new_count, p...  87.8 us
    all_to_all x1, blocking collectives, on_device(): parts = lax.all_to_all(parts, 'kv', split_axis=0, concat_axis=0, tiled=True)  71.4 us
    all_to_all x1, blocking collectives, on_device(): lax.all_to_all(hidden_sum, 'req', split_axis=0, concat_axis=0, tiled=True)  39.8 us
    all_gather x1, waiting for transfers between devices, on_device(): moe_in = lax.all_gather(moe_rows, ('req', 'kv'), axis=0, tiled=True)  37.7 us
    all_gather x1, blocking collectives, on_device(): all_gates = lax.all_gather(expert_gates, 'req', axis=0, tiled=True)  30.7 us
    reduce_scatter x1, waiting for transfers between devices, on_device(): lax.psum_scatter(partial_out.astype(jnp.bfloat16), 'kv', scatter_dimensio...  29.8 us
    dot_general x1, matrix products, on_device(): jnp.dot(jnp.concatenate(hidden, axis=1), w_down.reshape(experts_dev * hid...  19.4 us
    dot_general x2, matrix products, on_device(): jnp.dot(moe_in, w_gate_up[expert, 1], preferred_element_type=jnp.float32)  19.2 us
  transfers between devices with their start and end apart: 2, of which 2 were waited for; matrix products, arithmetic and copies ran while one was open for 0% of the time, Pallas kernels for 0%

profile of v2, /device:TPU:0, one launch (start us, length us, event | category | flops | bytes accessed | tf_op | source)
XLA Modules:
  0.0 412.1 jit_solution(4106305234957990431)
XLA Ops:
  6.5 1.5 fusion.19
  8.1 10.5 %copy.41 = bf16[2880,1280]{0,1:T(8,128)(2,1)} copy(bf16[2880,1280]{1,0:T(8,128)(2,1)} %param.15) | data formatting | bytes 14745600 | tf_op args[2]
  18.6 5.4 %fusion.23 = f32[128,2,10,64]{0,3,2,1:T(8,128)S(1)} fusion(bf16[2,10,64,2880]{3,2,1,0:T(8,128)(2,1)} %bitcast.80, bf16[1,128,2880]{1,2,0:T(8,128)(2,1)S(1)} %copy-done.2, f32[2880]{0:T(1024)S(1)} %copy-done.4, f32[128]{0:T(128)S(1)} %add_rsqrt_fusion.1), kind=kOutput, calls=%fused_computation.26 | convolution fusion | flops 945192960 | bytes 8777472 | tf_op jit(solution)/shard_map/dot_general | solution.py:200
  24.8 0.1 reshape.177
  24.8 0.1 broadcast_bitcast_fusion
  24.9 0.1 multiply_cosine_fusion
  25.1 0.1 subtract_convert_fusion
  25.2 0.1 copy.49.fresh_ref
  25.4 3.4 copy-done
  28.8 87.8 %cache_attention.1 = bf16[2,64,1024]{2,1,0:T(8,128)(2,1)S(1)} custom-call(s32[128]{0:T(128)S(1)} %bitcast.79, s32[1]{0:T(128)} %copy.59.length_ref, bf16[2,128,1024]{2,1,0:T(8,128)(2,1)S(1)} %concatenate.17.query_ref, bf16[128,256]{1,0:T(8,128)(2,1)S(1)} %copy.49.fresh_ref, f32[2,1024]{1,0:T(2,128)S(1)} %bitcast.78, bf16[128,128,256]{2,1,0:T(8,128)(2,1)S(1)} %copy-done, ...), custom_call_target="tpu_custom_call" | custom-call | tf_op jit(solution)/shard_map/cache_attention/pallas_call | solution.py:139
  116.6 0.1 copy_bitcast_fusion.1
  116.6 5.7 %convolution_convert_fusion.1 = bf16[128,2880]{1,0:T(8,128)(2,1)} fusion(bf16[128,1024]{0,1:T(8,128)(2,1)S(1)} %bitcast.82, bf16[1024,2880]{0,1:T(8,128)(2,1)} %param.17), kind=kOutput, calls=%fused_computation.13 | convolution fusion | flops 755343360 | bytes 6897664 | tf_op jit(solution)/shard_map/dot_general | solution.py:217
  122.4 0.0 all-gather.2.cloned.1.call-start
  122.4 0.3 constant_dynamic-slice_fusion.2
  122.7 0.3 copy.50
  123.0 29.8 %reduce-scatter.2.cloned.1.call-done = bf16[32,2880]{1,0:T(8,128)(2,1)} async-done(((bf16[128,2880]{1,0:T(8,128)(2,1)}), bf16[32,2880]{1,0:T(8,128)(2,1)}) %reduce-scatter.2.cloned.1.call-update) | async-done | bytes 184336 | tf_op jit(solution)/shard_map/reduce_scatter | solution.py:218
  152.8 1.1 multiply_reduce_fusion
  153.9 1.7 multiply_convert_fusion.2
  155.7 30.7 %all_gather.7 = f32[1024,16]{0,1:T(8,128)S(1)} all-gather(f32[128,16]{0,1:T(8,128)S(1)} %select_reduce_fusion), channel_id=1, replica_groups=mesh['req'=8,'kv'=4] {'req'}, dimensions={0}, use_global_device_ids=true | all-gather | bytes 73728 | tf_op jit(solution)/shard_map/all_gather | solution.py:194
  186.4 37.7 %all-gather.2.cloned.1.call-done = bf16[1024,2880]{1,0:T(8,128)(2,1)} async-done(((bf16[32,2880]{1,0:T(8,128)(2,1)}), bf16[1024,2880]{1,0:T(8,128)(2,1)}) %all-gather.2.cloned.1.call-update) | async-done | bytes 5898256 | tf_op jit(solution)/shard_map/all_gather | solution.py:224
  224.1 10.5 %fusion = f32[1024,720]{0,1:T(8,128)} fusion(bf16[1024,2880]{1,0:T(8,128)(2,1)} %all-gather.2.cloned.1.call-done, bf16[2,2,2880,720]{2,3,1,0:T(8,128)(2,1)} %param.24), kind=kOutput, calls=%fused_computation.1 | convolution fusion | flops 4246732800 | bytes 13217792 | tf_op jit(solution)/shard_map/dot_general | solution.py:228
  234.7 8.7 %fusion.4 = f32[1024,720]{0,1:T(8,128)} fusion(bf16[1024,2880]{1,0:T(8,128)(2,1)S(1)} %copy-done.8, bf16[2,2,2880,720]{2,3,1,0:T(8,128)(2,1)} %param.24), kind=kOutput, calls=%fused_computation.5 | convolution fusion | flops 4246732800 | bytes 13086720 | tf_op jit(solution)/shard_map/dot_general | solution.py:228
  243.4 7.3 %multiply_convert_fusion = bf16[1024,720]{0,1:T(8,128)(2,1)S(1)} fusion(f32[1024,720]{0,1:T(8,128)} %fusion, bf16[1024,2880]{1,0:T(8,128)(2,1)S(1)} %copy-done.8, bf16[2,2,2880,720]{2,3,1,0:T(8,128)(2,1)S(1)} %bitcast.89, f32[1024]{0:T(1024)S(1)} %bitcast.85), kind=kOutput, calls=%fused_computation.18 | convolution fusion | flops 4253368320 | bytes 14696448 | tf_op jit(solution)/shard_map/dot_general | solution.py:227
  250.7 7.1 %multiply_convert_fusion.1 = bf16[1024,720]{0,1:T(8,128)(2,1)S(1)} fusion(f32[1024,720]{0,1:T(8,128)} %fusion.4, bf16[1024,2880]{1,0:T(8,128)(2,1)S(1)} %copy-done.8, bf16[2,2,2880,720]{2,3,1,0:T(8,128)(2,1)S(1)} %bitcast.89, f32[1024]{0:T(1024)S(1)} %bitcast.84), kind=kOutput, calls=%fused_computation.19 | convolution fusion | flops 4253368320 | bytes 14696448 | tf_op jit(solution)/shard_map/dot_general | solution.py:227
  257.7 19.4 %convolution_convert_fusion = bf16[1024,2880]{0,1:T(8,128)(2,1)} fusion(bf16[1440,2880]{1,0:T(8,128)(2,1)} %bitcast.90, bf16[1024,720]{0,1:T(8,128)(2,1)S(1)} %multiply_convert_fusion, bf16[1024,720]{0,1:T(8,128)(2,1)S(1)} %multiply_convert_fusion.1), kind=kOutput, calls=%fused_computation | convolution fusion | flops 8502312960 | bytes 17141760 | tf_op jit(solution)/shard_map/dot_general | solution.py:231
  277.1 8.5 %copy.46 = bf16[1024,2880]{1,0:T(8,128)(2,1)} copy(bf16[1024,2880]{0,1:T(8,128)(2,1)} %convolution_convert_fusion) | data formatting | bytes 11796480 | tf_op jit(solution)/shard_map/convert_element_type | solution.py:235
  285.6 3.3 copy.47
  288.9 71.4 %all_to_all.10 = bf16[4,8,32,2880]{3,2,1,0:T(8,128)(2,1)} all-to-all(bf16[4,8,32,2880]{3,2,1,0:T(8,128)(2,1)S(1)} %copy.47), channel_id=1, replica_groups=mesh['req'=8,'kv'=4] {'kv'}, dimensions={0} | all-to-all | bytes 11796480 | tf_op jit(solution)/shard_map/all_to_all | solution.py:237
  360.4 4.2 %reduce_sum.51 = bf16[8,32,2880]{2,1,0:T(8,128)(2,1)S(1)} reduce(bf16[4,8,32,2880]{3,2,1,0:T(8,128)(2,1)} %all_to_all.10, bf16[]{:T(256)} %constant.16.clone.1), dimensions={0}, to_apply=%region_4.5 | reduce | flops 2211840 | bytes 7372802 | tf_op jit(solution)/shard_map/reduce_sum | solution.py:238
  364.6 39.8 %all_to_all.11 = bf16[8,32,2880]{2,1,0:T(8,128)(2,1)S(1)} all-to-all(bf16[8,32,2880]{2,1,0:T(8,128)(2,1)S(1)} %reduce_sum.51), channel_id=1, replica_groups=mesh['req'=8,'kv'=4] {'req'}, dimensions={0} | all-to-all | bytes 2949120 | tf_op jit(solution)/shard_map/all_to_all | solution.py:239
  404.3 0.2 convert_reduce_fusion
  404.5 0.7 fusion.28
  (46 shorter events, 0.3 us)
Async XLA Ops:
  6.5 146.2 %reduce-scatter.2.cloned.1.call-start = ((), (), s32[]{:S(2)}) async-start(), calls=%async_computation.3 | async-start | bytes 942080 | tf_op jit(solution)/shard_map/reduce_scatter | solution.py:218
  8.1 10.5 %copy-start.2 = (bf16[1,128,2880]{1,2,0:T(8,128)(2,1)S(1)}, bf16[1,128,2880]{1,2,0:T(8,128)(2,1)}, u32[]{:S(2)}) copy-start(bf16[1,128,2880]{1,2,0:T(8,128)(2,1)} %param.13) | copy-start | bytes 2211844
  8.1 10.5 %copy-start.4 = (f32[2880]{0:T(1024)S(1)}, f32[2880]{0:T(1024)}, u32[]{:S(2)}) copy-start(f32[2880]{0:T(1024)} %param.14) | copy-start | bytes 34564
  18.6 6.1 %copy-start.9 = (f32[16]{0:T(128)S(1)}, f32[16]{0:T(128)}, u32[]{:S(2)}) copy-start(f32[16]{0:T(128)} %param.16) | copy-start | bytes 196
  18.6 6.8 %copy-start.1 = (s32[1,128]{1,0:T(1,128)S(1)}, s32[1,128]{1,0:T(1,128)}, u32[]{:S(2)}) copy-start(s32[1,128]{1,0:T(1,128)} %param.19) | copy-start | bytes 1540
  25.4 3.4 copy-start
  122.3 31.5 %copy-start.5 = (f32[2880]{0:T(1024)S(1)}, f32[2880]{0:T(1024)}, u32[]{:S(2)}) copy-start(f32[2880]{0:T(1024)} %param.21) | copy-start | bytes 34564
  122.3 33.3 %copy-start.6 = (f32[1,128,4]{1,2,0:T(4,128)S(1)}, f32[1,128,4]{1,2,0:T(4,128)}, u32[]{:S(2)}) copy-start(f32[1,128,4]{1,2,0:T(4,128)} %param.23) | copy-start | bytes 6148
  122.3 33.3 %copy-start.7 = (s32[1,128,4]{1,2,0:T(4,128)S(1)}, s32[1,128,4]{1,2,0:T(4,128)}, u32[]{:S(2)}) copy-start(s32[1,128,4]{1,2,0:T(4,128)} %param.22) | copy-start | bytes 6148
  122.4 101.8 %all-gather.2.cloned.1.call-start = ((), (), s32[]{:S(2)}) async-start(), calls=%async_computation.4 | async-start | bytes 6217728 | tf_op jit(solution)/shard_map/all_gather | solution.py:224
  224.1 10.5 %copy-start.8 = (bf16[1024,2880]{1,0:T(8,128)(2,1)S(1)}, bf16[1024,2880]{1,0:T(8,128)(2,1)}, u32[]{:S(2)}) copy-start(bf16[1024,2880]{1,0:T(8,128)(2,1)} %all-gather.2.cloned.1.call-done) | copy-start | bytes 17694724
  224.1 19.2 %slice-start = ((s8[16957440]{0:T(1024)(128)(4,1)}), s8[4194304]{0:T(1024)(128)(4,1)S(1)}, s32[]{:S(2)}) async-start(s8[16957440]{0:T(1024)(128)(4,1)} %bitcast.88), calls=%async_computation.5 | async-start | bytes 8388608
  224.1 19.2 %slice-start.1 = ((s8[16957440]{0:T(1024)(128)(4,1)}), s8[4194304]{0:T(1024)(128)(4,1)S(1)}, s32[]{:S(2)}) async-start(s8[16957440]{0:T(1024)(128)(4,1)} %bitcast.88), calls=%async_computation.6 | async-start | bytes 8388608
  224.1 19.2 %slice-start.2 = ((s8[16957440]{0:T(1024)(128)(4,1)}), s8[4194304]{0:T(1024)(128)(4,1)S(1)}, s32[]{:S(2)}) async-start(s8[16957440]{0:T(1024)(128)(4,1)} %bitcast.88), calls=%async_computation.7 | async-start | bytes 8388608
  234.7 8.7 %slice-start.3 = ((s8[16957440]{0:T(1024)(128)(4,1)}), s8[4194304]{0:T(1024)(128)(4,1)S(1)}, s32[]{:S(2)}) async-start(s8[16957440]{0:T(1024)(128)(4,1)} %bitcast.88), calls=%async_computation.8 | async-start | bytes 8388608
  234.7 8.7 %slice-start.4 = ((s8[16957440]{0:T(1024)(128)(4,1)}), s8[180224]{0:T(1024)(128)(4,1)S(1)}, s32[]{:S(2)}) async-start(s8[16957440]{0:T(1024)(128)(4,1)} %bitcast.88), calls=%async_computation.9 | async-start | bytes 360448
  364.6 40.0 %copy-start.3 = (bf16[32,2880]{1,0:T(8,128)(2,1)S(1)}, bf16[32,2880]{1,0:T(8,128)(2,1)}, u32[]{:S(2)}) copy-start(bf16[32,2880]{1,0:T(8,128)(2,1)} %reduce-scatter.2.cloned.1.call-done) | copy-start | bytes 552964
Sparse Core Ops, SparseCore 0:
  122.5 30.2 reduce-scatter.1
  156.0 68.0 all-gather.1
